TPU v7x, 32 devices: a whole 2x2x4 slice. The times are simulated.
32 devices in a mesh: groups: 2 (over y), tm: 4 (over z), head: 2 (over x), batch: 2 (over core).
Axes of the slice: x: 2, y: 2, z: 4, core: 2. Of those that a mesh axis runs over, the one named last changes fastest.
Arguments:
- u_input: bfloat16 [4, 1024, 1536], P(('groups', 'batch'), 'tm'), parts along dimension 0, may hold values from -6 to 6
- head_values: bfloat16 [4, 1024, 3072], P(('groups', 'batch'), 'tm', 'head'), parts along dimension 0, may hold values from -6 to 6
- grad_output: bfloat16 [4, 1024, 3072], P(('groups', 'batch'), 'tm', 'head'), parts along dimension 0, may hold values from -6 to 6
- w_bc: bfloat16 [1536, 256], replicated, may hold values from -0.15625 to 0.15625
- w_dt: bfloat16 [1536, 48], P(None, 'head'), may hold values from -0.15625 to 0.15625
- dt_bias: float32 [48], P('head'), may hold values from -1.5 to 0.5
- a_log: float32 [48], P('head'), as said below
Outputs:
- grad_input: bfloat16 [4, 1024, 1536], P(('groups', 'batch'), 'tm'), parts along dimension 0
- grad_values: bfloat16 [4, 1024, 3072], P(('groups', 'batch'), 'tm', 'head'), parts along dimension 0
- grad_w_bc: float32 [3072, 256], P(('groups', 'tm', 'batch')), parts along dimension 0
- grad_w_dt: float32 [3072, 48], P('groups', 'head'), parts along dimension 0
- grad_dt_bias: float32 [96], P(('groups', 'head')), parts along dimension 0
- grad_a_log: float32 [96], P(('groups', 'head')), parts along dimension 0
There are 2 independent parts, one for each index of `groups`. A program takes and returns all parts, laid end to end along the dimension named above; an argument that names none is the same for every part. Nothing has to cross between parts.
Inputs may be any that keep to these rules, and one draw needn't show every extreme that they name: a_log lies between log(0.3 / 1024) and log(0.08).
All inputs are finite; a program needn't handle non-finite values.
Results may differ from a plain program's by a relative error of at most 0.0059.
Values may be sent and summed in bfloat16 or wider, within the bound.
A program may use at most 64 MiB of HBM per device.

v0:
```python
import jax
import jax.numpy as jnp
from jax import lax
from jax.sharding import PartitionSpec as P


def prefix(shard, axis, combine, identity, reverse):
    length, place = (lax.axis_size(axis), lax.axis_index(axis))
    everything = jax.tree.map(lambda part: lax.all_gather(part, axis), shard)
    start = jax.tree.map(
        lambda part, zero: jnp.broadcast_to(jnp.asarray(zero, part.dtype), part.shape),
        shard,
        identity,
    )

    def turn(k, before):
        at = length - 1 - k if reverse else k
        reached = at > place if reverse else at < place
        new = combine(before, jax.tree.map(lambda part: part[at], everything))
        return jax.tree.map(lambda a, b: jnp.where(reached, a, b), new, before)

    return lax.fori_loop(0, length, turn, start)


def span_core(b_rows, c_rows, time_step, values_in, rate, state_in):
    highest = lax.Precision.HIGHEST
    log_decay = jnp.cumsum(time_step * rate[None, :], axis=0)
    length_t = time_step.shape[0]
    causal = jnp.arange(length_t)[:, None] >= jnp.arange(length_t)[None, :]
    differ = log_decay.T[:, :, None] - log_decay.T[:, None, :]
    decay = jnp.exp(jnp.where(causal[None], differ, -jnp.inf))
    scores = jnp.dot(c_rows, b_rows.T, precision=highest)
    mixing = decay * scores[None] * time_step.T[:, None, :]
    inner = jnp.einsum("hts,shp->thp", mixing, values_in, precision=highest)
    carried = jnp.exp(log_decay)[:, :, None] * jnp.einsum(
        "tn,hpn->thp", c_rows, state_in, precision=highest
    )
    output = inner + carried
    tail_w = jnp.exp(log_decay[-1][None, :] - log_decay) * time_step
    final = jnp.exp(log_decay[-1])[:, None, None] * state_in + jnp.einsum(
        "sh,shp,sn->hpn", tail_w, values_in, b_rows, precision=highest
    )
    return (output, final)


def combine_maps(earlier, later):
    return (earlier[0] * later[0], later[0][..., None, None] * earlier[1] + later[1])


def on_device(u_input, head_values, grad_output, w_bc, w_dt, dt_bias, a_log):
    highest = lax.Precision.HIGHEST
    seq_count, token_count, width = u_input.shape
    heads = w_dt.shape[1]
    state_size = w_bc.shape[1] // 2
    head_size = head_values.shape[2] // heads
    rate = -jnp.exp(a_log)
    flat = u_input.reshape(seq_count * token_count, width)
    proj = jnp.dot(flat, w_bc, preferred_element_type=jnp.float32).astype(jnp.bfloat16)
    pre = jnp.dot(flat, w_dt, preferred_element_type=jnp.float32) + dt_bias[None, :]
    delta = jax.nn.softplus(pre).reshape(seq_count, token_count, heads)
    b_all = proj[:, :state_size].astype(jnp.float32).reshape(seq_count, token_count, state_size)
    c_all = proj[:, state_size:].astype(jnp.float32).reshape(seq_count, token_count, state_size)
    values_all = head_values.astype(jnp.float32).reshape(seq_count, token_count, heads, head_size)
    cotangent = grad_output.astype(jnp.float32).reshape(seq_count, token_count, heads, head_size)

    def summarize(b_rows, c_rows, time_step, values_in, grads_in):
        log_decay = jnp.cumsum(time_step * rate[None, :], axis=0)
        tail_w = jnp.exp(log_decay[-1][None, :] - log_decay) * time_step
        own_state = jnp.einsum("sh,shp,sn->hpn", tail_w, values_in, b_rows, precision=highest)
        pulled = jnp.einsum(
            "th,thp,tn->hpn", jnp.exp(log_decay), grads_in, c_rows, precision=highest
        )
        return (jnp.exp(log_decay[-1]), own_state, pulled)

    decays, own_states, pulls = jax.vmap(summarize)(b_all, c_all, delta, values_all, cotangent)
    unit = (jnp.ones_like(decays), jnp.zeros_like(own_states))
    incoming = prefix((decays, own_states), "tm", combine_maps, unit, False)[1]
    outgoing = prefix((decays, pulls), "tm", combine_maps, unit, True)[1]

    def backward_one(b_rows, c_rows, time_step, values_in, grads_in, state_in, state_grad):
        _, pull_back = jax.vjp(span_core, b_rows, c_rows, time_step, values_in, rate, state_in)
        return pull_back((grads_in, state_grad))

    g_b, g_c, g_delta, g_x, g_rate, _ = jax.vmap(backward_one)(
        b_all, c_all, delta, values_all, cotangent, incoming, outgoing
    )
    partial_proj = jnp.concatenate([g_b, g_c], axis=-1).reshape(
        seq_count * token_count, 2 * state_size
    )
    grad_proj = lax.psum(partial_proj, "head").astype(jnp.bfloat16)
    grad_pre = g_delta.reshape(seq_count * token_count, heads) * jax.nn.sigmoid(pre)
    grad_pre_b = grad_pre.astype(jnp.bfloat16)
    from_bc = jnp.dot(grad_proj, w_bc.T, preferred_element_type=jnp.float32)
    all_pre, all_w_dt = (
        lax.all_gather(grad_pre_b, "head", axis=1, tiled=True),
        lax.all_gather(w_dt, "head", axis=1, tiled=True),
    )
    grad_input = from_bc + jnp.dot(all_pre, all_w_dt.T, preferred_element_type=jnp.float32)
    grad_input = grad_input.astype(jnp.bfloat16).reshape(seq_count, token_count, width)
    grad_values = g_x.reshape(seq_count, token_count, heads * head_size).astype(jnp.bfloat16)
    local_w_dt = jnp.einsum("td,th->dh", flat, grad_pre_b, preferred_element_type=jnp.float32)
    grad_w_dt, grad_dt_bias, grad_a_log = lax.psum(
        (local_w_dt, jnp.sum(grad_pre, axis=0), jnp.sum(g_rate, axis=0) * rate), ("tm", "batch")
    )
    local_w_bc = jnp.einsum("td,tk->dk", flat, grad_proj, preferred_element_type=jnp.float32)
    grad_w_bc = lax.psum_scatter(local_w_bc, ("tm", "batch"), scatter_dimension=0, tiled=True)
    return (grad_input, grad_values, grad_w_bc, grad_w_dt, grad_dt_bias, grad_a_log)


def solution(mesh):
    return jax.shard_map(
        on_device,
        mesh=mesh,
        in_specs=(
            P(("groups", "batch"), "tm", None),
            P(("groups", "batch"), "tm", "head"),
            P(("groups", "batch"), "tm", "head"),
            P(),
            P(None, "head"),
            P("head"),
            P("head"),
        ),
        out_specs=(
            P(("groups", "batch"), "tm", None),
            P(("groups", "batch"), "tm", "head"),
            P(("groups", "tm", "batch"), None),
            P("groups", "head"),
            P(("groups", "head")),
            P(("groups", "head")),
        ),
        check_vma=False,
    )
```

profile of v0, /device:TPU:0, one launch (start us, length us, event | category | flops | bytes accessed | tf_op | source)
XLA Modules:
  0.0 287.1 jit_solution(3803811651553812673)
XLA Ops:
  13.4 1.8 fusion.20
  16.7 12.8 %all_gather.24 = f32[4,1,24]{2,1,0:T(1,128)} all-gather(f32[1,1,24]{2,1,0:T(1,128)S(1)} %get-tuple-element.385), channel_id=1, replica_groups=mesh['groups'=2,'tm'=4,'head'=2,'batch'=2] {'tm'}, dimensions={0}, use_global_device_ids=true | all-gather | bytes 480 | tf_op jit(solution)/shard_map/all_gather | solution.py:9
  29.5 52.0 %all-gather.5.cloned.1.call-done = f32[96,64,128]{2,1,0:T(8,128)} async-done(((f32[24,64,128]{2,1,0:T(8,128)}), f32[96,64,128]{2,1,0:T(8,128)}) %all-gather.5.cloned.1.call-update) | async-done | bytes 3145744 | tf_op jit(solution)/shard_map/all_gather | solution.py:9
  81.6 7.8 %while.30 = (s32[]{:T(128)}, f32[1,24,64,128]{3,2,1,0:T(8,128)S(1)}, s32[]{:T(128)}, f32[4,1,24]{2,1,0:T(1,128)}, f32[4,1,24,64,128]{4,3,2,1,0:T(8,128)}, /*index=5*/s32[]{:T(128)}, s32[]{:T(128)}, s32[]{:T(128)}, s32[]{:T(128)}) while((s32[]{:T(128)}, f32[1,24,64,128]{3,2,1,0:T(8,128)S(1)}, s32[]{:T(128)}, f32[4,1,24]{2,1,0:T(1,128)}, ...), condition=%wide.region_3.4_spmd.clone, body=%wide.region_2.3_spmd.clone.sunk | while | flops 786440 | bytes 2359751 | solution.py:22
  89.4 2.5 fusion.18
  91.9 1.5 copy.111
  93.4 2.2 fusion.61
  95.6 1.6 copy.90
  97.2 2.5 fusion.16
  101.3 2.0 bitcast_multiply_fusion.1
  104.0 1.6 copy.112
  105.6 1.6 copy.95
  108.2 6.4 %fusion.7 = (f32[24,256]{1,0:T(8,128)}, f32[24,256]{1,0:T(8,128)}, f32[24,256]{1,0:T(8,128)}, f32[256,256]{1,0:T(8,128)}) fusion(f32[256,256]{1,0:T(8,128)S(1)} %fusion.53, f32[24,256]{1,0:T(8,128)} %copy.95, f32[24,256]{1,0:T(8,128)S(1)} %bitcast_add_fusion.8, pred[256,256]{1,0:T(8,128)(4,1)S(1)} %iota_compare_fusion, ...), kind=kOutput, calls=%fused_computation.14 | convolution fusion | flops 221689856 | bytes 2285568 | tf_op jit(solution)/shard_map/vmap(transpose(jvp(hts,shp->thp)))/dot_general | solution.py:34
  114.6 1.5 copy.100
  116.1 1.5 copy.99
  117.6 1.5 copy.97
  120.3 3.3 %fusion.25 = f32[1,256,128]{1,2,0:T(8,128)} fusion(f32[1,256,128]{1,2,0:T(8,128)S(1)} %convolution_bitcast_fusion.3, bf16[256,24,64]{0,2,1:T(8,128)(2,1)} %bitcast.249, f32[1,24,64,128]{3,2,1,0:T(8,128)S(1)} %get-tuple-element.232, f32[256,24]{0,1:T(8,128)} %copy.90), kind=kOutput, calls=%fused_computation.42 | convolution fusion | flops 604798976 | bytes 1859584 | tf_op jit(solution)/shard_map/vmap(transpose(jvp(sh,shp,sn->hpn)))/dot_general | solution.py:40
  123.6 38.5 %all-gather.7.cloned.1.call-done = f32[96,64,128]{2,1,0:T(8,128)} async-done(((f32[24,64,128]{2,1,0:T(8,128)}), f32[96,64,128]{2,1,0:T(8,128)}) %all-gather.7.cloned.1.call-update) | async-done | bytes 3145744 | tf_op jit(solution)/shard_map/all_gather | solution.py:9
  162.1 7.8 %while.31 = (s32[]{:T(128)}, f32[1,24,64,128]{3,2,1,0:T(8,128)S(1)}, s32[]{:T(128)}, f32[4,1,24]{2,1,0:T(1,128)}, f32[4,1,24,64,128]{4,3,2,1,0:T(8,128)}, /*index=5*/s32[]{:T(128)}, s32[]{:T(128)}) while((s32[]{:T(128)}, f32[1,24,64,128]{3,2,1,0:T(8,128)S(1)}, s32[]{:T(128)}, f32[4,1,24]{2,1,0:T(1,128)}, ...), condition=%wide.region_6.7_spmd.clone, body=%wide.region_5.6_spmd.clone.sunk | while | flops 786436 | bytes 2359689 | solution.py:22
  171.4 2.5 reduce-window.16
  174.1 2.9 %convolution_bitcast_fusion.2 = f32[256,128]{0,1:T(8,128)S(1)} fusion(f32[256,24,64]{0,2,1:T(8,128)} %bitcast.250, f32[1,24,64,128]{3,2,1,0:T(8,128)S(1)} %get-tuple-element.233), kind=kOutput, calls=%fused_computation.40 | convolution fusion | flops 603979776 | bytes 2490368 | tf_op jit(solution)/shard_map/vmap(transpose(jvp(tn,hpn->thp)))/dot_general | solution.py:35
  177.4 11.5 %all-reduce.7 = bf16[256,256]{0,1:T(8,128)(2,1)S(1)} all-reduce(f32[256,256]{0,1:T(8,128)S(1)} %maximum_bitcast_fusion), channel_id=1, replica_groups=mesh['groups'=2,'tm'=4,'head'=2,'batch'=2] {'head'}, use_global_device_ids=true, to_apply=%region_7.8 | all-reduce | flops 65536 | bytes 393216 | tf_op jit(solution)/shard_map/psum | solution.py:90
  190.5 1.5 convolution_bitcast_fusion
  192.0 3.0 %copy.113 = f32[1536,256]{1,0:T(8,128)} copy(f32[1536,256]{0,1:T(8,128)} %convolution_bitcast_fusion) | data formatting | bytes 3145728
  195.9 5.0 %all_gather.30 = bf16[1536,48]{0,1:T(8,128)(2,1)S(1)} all-gather(bf16[1536,24]{0,1:T(8,128)(2,1)S(1)} %copy-done.12), channel_id=1, replica_groups=mesh['groups'=2,'tm'=4,'head'=2,'batch'=2] {'head'}, dimensions={1}, use_global_device_ids=true | all-gather | bytes 221184 | tf_op jit(solution)/shard_map/all_gather | solution.py:96
  201.0 6.0 %fusion.19 = bf16[1,256,24,64]{1,3,2,0:T(8,128)(2,1)} fusion(f32[24,64,256]{2,1,0:T(8,128)} %get-tuple-element.387, bf16[24,64,256]{2,1,0:T(8,128)(2,1)S(1)} %bitcast.245, f32[256,256]{1,0:T(8,128)S(1)} %copy-done.14, f32[24,256]{1,0:T(8,128)S(1)} %copy-done.19, f32[24,256]{1,0:T(8,128)S(1)} %copy-done.21, pred[256,256]{1,0:T(8,128)(4,1)S(1)} %copy-done.18, ...), kind=kOutput, calls=%fused_computation.32 | convolution fusion | flops 1215430656 | bytes 3547136 | tf_op jit(solution)/shard_map/vmap(transpose(jvp(hts,shp->thp)))/dot_general | solution.py:34
  207.0 2.4 copy.104
  209.6 14.1 %all-reduce.2 = (f32[24]{0:T(128)}, f32[24]{0:T(128)}) all-reduce(f32[24]{0:T(128)S(1)} %copy-done.25, f32[24]{0:T(128)S(1)} %fusion.63), channel_id=1, replica_groups=mesh['groups'=2,'tm'=4,'head'=2,'batch'=2] {'tm','batch'}, use_global_device_ids=true, to_apply=%region_19.20 | all-reduce | flops 48 | bytes 384 | tf_op jit(solution)/shard_map/psum | solution.py:102
  223.7 4.4 %all_gather.29 = bf16[256,48]{0,1:T(8,128)(2,1)S(1)} all-gather(bf16[256,24]{0,1:T(8,128)(2,1)S(1)} %copy.103), channel_id=1, replica_groups=mesh['groups'=2,'tm'=4,'head'=2,'batch'=2] {'head'}, dimensions={1}, use_global_device_ids=true | all-gather | bytes 36864 | tf_op jit(solution)/shard_map/all_gather | solution.py:95
  229.8 10.8 %all-reduce.6.cloned.1.call-done = f32[1536,24]{0,1:T(8,128)} async-done(((f32[1536,24]{0,1:T(8,128)}), f32[1536,24]{0,1:T(8,128)}) %all-reduce.6.cloned.1.call-update) | async-done | bytes 147472 | tf_op jit(solution)/shard_map/psum | solution.py:102
  240.6 38.4 %reduce-scatter.4.cloned.1.call-done = f32[192,256]{1,0:T(8,128)} async-done(((f32[1536,256]{1,0:T(8,128)}), f32[192,256]{1,0:T(8,128)}) %reduce-scatter.4.cloned.1.call-update) | async-done | bytes 196624
  279.0 1.6 copy.132
  (120 shorter events, 33.9 us)
Async XLA Ops:
  7.2 1.2 copy-start
  7.2 5.1 %copy-start.2 = (bf16[1536,256]{1,0:T(8,128)(2,1)S(1)}, bf16[1536,256]{1,0:T(8,128)(2,1)}, u32[]{:S(2)}) copy-start(bf16[1536,256]{1,0:T(8,128)(2,1)} %param.14) | copy-start | bytes 2359300
  7.2 74.4 %all-gather.5.cloned.1.call-start = ((), (), s32[]{:S(2)}) async-start(), calls=%async_computation.2 | async-start | bytes 3932160 | tf_op jit(solution)/shard_map/all_gather | solution.py:9
  9.5 3.1 %copy-start.6 = (bf16[1,256,1536]{2,1,0:T(8,128)(2,1)S(1)}, bf16[1,256,1536]{2,1,0:T(8,128)(2,1)}, u32[]{:S(2)}) copy-start(bf16[1,256,1536]{2,1,0:T(8,128)(2,1)} %param.13) | copy-start | bytes 2359300
  10.9 0.6 copy-start.11
  12.6 0.7 copy-start.16
  15.2 146.9 %all-gather.7.cloned.1.call-start = ((), (), s32[]{:S(2)}) async-start(), calls=%async_computation.3 | async-start | bytes 3932160 | tf_op jit(solution)/shard_map/all_gather | solution.py:9
  16.7 80.5 %copy-start.1 = (bf16[1,256,1536]{1,2,0:T(8,128)(2,1)}, bf16[1,256,1536]{1,2,0:T(8,128)(2,1)S(1)}, u32[]{:S(2)}) copy-start(bf16[1,256,1536]{1,2,0:T(8,128)(2,1)S(1)} %copy.91) | copy-start | bytes 2359300
  99.8 140.8 %all-reduce.6.cloned.1.call-start = ((), (), s32[]{:S(2)}) async-start(), calls=%async_computation.1 | async-start | bytes 294912 | tf_op jit(solution)/shard_map/psum | solution.py:102
  107.2 7.4 %copy-start.17 = (pred[256,256]{1,0:T(8,128)(4,1)}, pred[256,256]{1,0:T(8,128)(4,1)S(1)}, u32[]{:S(2)}) copy-start(pred[256,256]{1,0:T(8,128)(4,1)S(1)} %iota_compare_fusion) | copy-start | bytes 196612
  108.0 6.6 %copy-start.20 = (f32[24,256]{1,0:T(8,128)}, f32[24,256]{1,0:T(8,128)S(1)}, u32[]{:S(2)}) copy-start(f32[24,256]{1,0:T(8,128)S(1)} %bitcast_add_fusion.8) | copy-start | bytes 73732
  108.2 6.4 %copy-start.13 = (f32[256,256]{1,0:T(8,128)}, f32[256,256]{1,0:T(8,128)S(1)}, u32[]{:S(2)}) copy-start(f32[256,256]{1,0:T(8,128)S(1)} %fusion.53) | copy-start | bytes 786436
  169.9 1.2 copy-start.24
  170.2 0.9 copy-start.4
  170.2 1.0 copy-start.9
  170.2 1.0 copy-start.10
  171.3 5.7 %copy-start.5 = (f32[256,256]{1,0:T(8,128)S(1)}, f32[256,256]{1,0:T(8,128)}, u32[]{:S(2)}) copy-start(f32[256,256]{1,0:T(8,128)} %get-tuple-element.353) | copy-start | bytes 786436
  174.0 3.4 %copy-start.7 = (f32[1,256,128]{1,2,0:T(8,128)S(1)}, f32[1,256,128]{1,2,0:T(8,128)}, u32[]{:S(2)}) copy-start(f32[1,256,128]{1,2,0:T(8,128)} %fusion.25) | copy-start | bytes 393220
  174.1 14.8 %copy-start.22 = (f32[24,2]{0,1:T(2,128)}, f32[24,2]{0,1:T(2,128)S(1)}, u32[]{:S(2)}) copy-start(f32[24,2]{0,1:T(2,128)S(1)} %slice_bitcast_fusion) | copy-start | bytes 580
  174.1 14.8 %copy-start.8 = (f32[24,256]{0,1:T(8,128)S(1)}, f32[24,256]{0,1:T(8,128)}, u32[]{:S(2)}) copy-start(f32[24,256]{0,1:T(8,128)} %copy.97) | copy-start | bytes 73732
  190.4 88.6 %reduce-scatter.4.cloned.1.call-start = ((), (), s32[]{:S(2)}) async-start(), calls=%async_computation.4 | async-start | bytes 1769472
  195.0 0.9 copy-start.12
  195.1 5.9 %copy-start.14 = (f32[256,256]{1,0:T(8,128)S(1)}, f32[256,256]{1,0:T(8,128)}, u32[]{:S(2)}) copy-start(f32[256,256]{1,0:T(8,128)} %copy-done.13) | copy-start | bytes 786436
  195.1 5.9 %copy-start.15 = (f32[256,24]{0,1:T(8,128)S(1)}, f32[256,24]{0,1:T(8,128)}, u32[]{:S(2)}) copy-start(f32[256,24]{0,1:T(8,128)} %copy.90) | copy-start | bytes 73732
  195.1 5.9 %copy-start.18 = (pred[256,256]{1,0:T(8,128)(4,1)S(1)}, pred[256,256]{1,0:T(8,128)(4,1)}, u32[]{:S(2)}) copy-start(pred[256,256]{1,0:T(8,128)(4,1)} %copy-done.17) | copy-start | bytes 196612
  195.1 5.9 %copy-start.19 = (f32[24,256]{1,0:T(8,128)S(1)}, f32[24,256]{1,0:T(8,128)}, u32[]{:S(2)}) copy-start(f32[24,256]{1,0:T(8,128)} %copy.95) | copy-start | bytes 73732
  195.1 5.9 %copy-start.21 = (f32[24,256]{1,0:T(8,128)S(1)}, f32[24,256]{1,0:T(8,128)}, u32[]{:S(2)}) copy-start(f32[24,256]{1,0:T(8,128)} %copy-done.20) | copy-start | bytes 73732
  207.0 2.4 copy-start.23
  207.0 2.6 copy-start.26
  207.0 2.6 copy-start.25
  207.0 21.1 %copy-start.3 = (bf16[1536,256]{1,0:T(8,128)(2,1)S(1)}, bf16[1536,256]{1,0:T(8,128)(2,1)}, u32[]{:S(2)}) copy-start(bf16[1536,256]{1,0:T(8,128)(2,1)} %param.14) | copy-start | bytes 2359300
Sparse Core Ops, SparseCore 0:
  15.3 66.1 all-gather.4
  99.9 62.1 all-gather.6
  190.6 49.9 all-reduce.5
  243.4 35.5 reduce-scatter.3
where the time goes:
time: 289 us; the launch traced here: 287 us
  waiting for transfers between devices  140 us (48%)
  blocking collectives  47.8 us (17%)
  matrix products  33.6 us (12%)
  local copies, waits for them, and re-layouts  30 us (10%)
  other arithmetic  21.3 us (7%)
  between operations  14.1 us (5%)
    all_gather x2, waiting for transfers between devices, prefix(): everything = jax.tree.map(lambda part: lax.all_gather(part, axis), shard)  90.5 us
    unnamed x5, waiting for transfers between devices  38.5 us
    psum x1, blocking collectives, on_device(): lax.psum((local_w_dt, jnp.sum(grad_pre, axis=0), jnp.sum(g_rate, axis=0)...  14.1 us
    all_gather x1, blocking collectives, prefix(): everything = jax.tree.map(lambda part: lax.all_gather(part, axis), shard)  12.8 us
    dot_general x2, matrix products, span_core(): inner = jnp.einsum('hts,shp->thp', mixing, values_in, precision=highest)  12.4 us
    psum x1, blocking collectives, on_device(): grad_proj = lax.psum(partial_proj, 'head').astype(jnp.bfloat16)  11.5 us
    psum x1, waiting for transfers between devices, on_device(): lax.psum((local_w_dt, jnp.sum(grad_pre, axis=0), jnp.sum(g_rate, axis=0)...  10.8 us
    unnamed x59, local copies, waits for them, and re-layouts  10.7 us
  transfers between devices with their start and end apart: 4, of which 4 were waited for; matrix products, arithmetic and copies ran while one was open for 14% of the time, Pallas kernels for 0%

commit v1 on v0

v1 whole, which is shorter than its diff:
```python
import functools

import jax
import jax.numpy as jnp
from jax import lax
from jax.experimental import pallas as pl
from jax.experimental.pallas import tpu as pltpu
from jax.sharding import PartitionSpec as P

MESH = pl.DeviceIdType.MESH
F32 = jnp.float32
BF16 = jnp.bfloat16
LANES = 128
NT = (((1,), (1,)), ((), ()))
TN = (((0,), (0,)), ((), ()))


def dot(a, b, dims=(((1,), (0,)), ((), ()))):
    return lax.dot_general(a, b, dims, preferred_element_type=F32)


def dot_exact(a, b):
    return lax.dot_general(
        a, b, (((1,), (0,)), ((), ())),
        precision=lax.Precision.HIGHEST, preferred_element_type=F32,
    )


def kernel(
    zn, hn, bn, heads, split,
    u, x, g, wbc, wdt, bias, alog,
    gin, gval, gwbc, gwdt, gsmall,
    wpad, rows, proj, l_t, l_sel, d_sel, xs, gs, own_f, own_b, gxi, st, dst, col_e, erows,
    direct, qd, gl, fin, gacc,
    sf, rf, sb, rb, wx, px, gpx, csend, crecv, plocal, zsend, zrecv, fsend, frecv,
    wsend, wrecv, wsum, wzsend, wzrecv, wfsend, wfrecv, smsend, smrecv, smzsend, smzrecv,
    f_ss, f_rs, b_ss, b_rs, h_ss, h_rs, c_ss, c_rs, z_ss, z_rs,
):
    z, hx, bt = lax.axis_index("tm"), lax.axis_index("head"), lax.axis_index("batch")
    tokens, width = u.shape
    pairs = heads // 2
    per = 2 if pairs % 2 == 0 else 1
    chunks = pairs // per
    stride = 2
    state = LANES
    rpad = wx.shape[1]
    half = width // bn
    lane = lax.broadcasted_iota(jnp.int32, (tokens, LANES), 1)
    lane1 = lax.broadcasted_iota(jnp.int32, (1, LANES), 1)
    low = lane < 64
    low1 = lane1 < 64

    barrier = pltpu.get_barrier_semaphore()
    for k in range(1, zn):
        pl.semaphore_signal(barrier, inc=1, device_id={"tm": lax.rem(z + k, zn)}, device_id_type=MESH)
    for k in range(1, hn):
        pl.semaphore_signal(barrier, inc=1, device_id={"head": lax.rem(hx + k, hn)}, device_id_type=MESH)
    for k in range(1, bn):
        pl.semaphore_signal(barrier, inc=1, device_id={"batch": lax.rem(bt + k, bn)}, device_id_type=MESH)

    wpad[...] = jnp.zeros_like(wpad)
    wpad[:, :heads] = wdt[...]
    rows[...] = jnp.zeros_like(rows)
    rows[0:1, :heads] = bias[...]
    rows[1:2, :heads] = alog[...]
    uu = u[...]
    proj[...] = dot(uu, wbc[...]).astype(BF16)
    pre = dot(uu, wpad[...]) + rows[0:1, :]
    delta = jnp.maximum(pre, 0.0) + jnp.log1p(jnp.exp(-jnp.abs(pre)))
    rate = -jnp.exp(rows[1:2, :])
    ti = lax.broadcasted_iota(jnp.int32, (tokens, tokens), 0)
    si = lax.broadcasted_iota(jnp.int32, (tokens, tokens), 1)
    log_decay = dot_exact((ti >= si).astype(F32), delta * rate)
    l_rows = log_decay.T
    for h in range(heads):
        l_t[h] = l_rows[h:h + 1, :]
    b_all, c_all = proj[:, :state], proj[:, state:]
    b_t = b_all.astype(F32).T.astype(BF16)
    c_t = c_all.astype(F32).T.astype(BF16)
    st[...] = jnp.where(ti <= si, dot(b_all, c_all, NT), 0.0)
    ident = (
        lax.broadcasted_iota(jnp.int32, (rpad, LANES), 0)
        == lax.broadcasted_iota(jnp.int32, (rpad, LANES), 1)
    ).astype(BF16)
    wx[hx] = dot(ident, wpad[...], NT).astype(BF16)

    def pick(value, head):
        return jnp.sum(jnp.where(lane == head, value, 0.0), axis=1, keepdims=True)

    def summarize(p, carry):
        cols = pl.ds(pl.multiple_of(p * LANES, LANES), LANES)
        ls = jnp.where(low, pick(log_decay, 2 * p), pick(log_decay, 2 * p + 1))
        ds = jnp.where(low, pick(delta, 2 * p), pick(delta, 2 * p + 1))
        l_sel[p] = ls
        d_sel[p] = ds
        xv = (jnp.exp(ls[tokens - 1:tokens, :] - ls) * ds * x[:, cols].astype(F32)).astype(BF16)
        gv = (jnp.exp(ls) * g[:, cols].astype(F32)).astype(BF16)
        xs[p] = xv
        gs[p] = gv
        own_f[p] = dot(b_t, xv)
        own_b[p] = dot(c_t, gv)
        return carry

    lax.fori_loop(0, pairs, summarize, 0)

    dst[...] = jnp.zeros_like(dst)
    erows[...] = jnp.zeros_like(erows)
    direct[...] = jnp.zeros_like(direct)
    qd[...] = jnp.zeros_like(qd)
    gl[...] = jnp.zeros_like(gl)
    fin[...] = jnp.zeros_like(fin)
    gacc[...] = jnp.zeros_like(gacc)

    @pl.when(z == 0)
    def _():
        rf[...] = jnp.zeros_like(rf)

    @pl.when(z == zn - 1)
    def _():
        rb[...] = jnp.zeros_like(rb)

    pl.semaphore_wait(barrier, zn + hn + bn - 3)

    def head_copies(k):
        to = {"head": lax.rem(hx + k, hn)}
        return [
            pltpu.make_async_remote_copy(
                ref.at[hx], ref.at[hx], h_ss.at[i, k], h_rs.at[i, k], device_id=to, device_id_type=MESH
            )
            for i, ref in enumerate((wx, px, gpx))
        ]

    for k in range(1, hn):
        head_copies(k)[0].start()

    def chain_f(c):
        part = pl.ds(c * per, per)
        return pltpu.make_async_remote_copy(
            sf.at[part], rf.at[part], f_ss.at[c], f_rs.at[c],
            device_id={"tm": lax.rem(z + 1, zn)}, device_id_type=MESH,
        )

    def chain_b(c):
        part = pl.ds(c * per, per)
        return pltpu.make_async_remote_copy(
            sb.at[part], rb.at[part], b_ss.at[c], b_rs.at[c],
            device_id={"tm": lax.rem(z + zn - 1, zn)}, device_id_type=MESH,
        )

    def chain_step(c, first, last, make, own, send, recv):
        @pl.when((c >= 0) & (c < chunks))
        def _():
            @pl.when(jnp.logical_not(first))
            def _():
                make(c).wait_recv()

            @pl.when(jnp.logical_not(last))
            def _():
                for j in range(per):
                    p = c * per + j
                    total = jnp.exp(l_sel[p, tokens - 1:tokens, :])
                    send[p] = (total * recv[p].astype(F32) + own[p]).astype(BF16)
                make(c).start()

    lm = low.astype(F32).astype(BF16)

    def local_pair(p):
        cols = pl.ds(pl.multiple_of(p * LANES, LANES), LANES)
        gb = g[:, cols]
        xb = x[:, cols]
        sh = tokens // 2
        for s0 in (0, sh):
            t0 = s0
            gx = []
            gt = gb[t0:, :]
            sm = st[s0:s0 + sh, t0:]
            add = jnp.zeros((sh, tokens - t0), F32)
            zero = [jnp.zeros((1, t0), F32)] if t0 else []
            dr = direct[s0:s0 + sh, :]
            for j in range(2):
                keep = lm[s0:s0 + sh, :]
                xm = xb[s0:s0 + sh, :] * (keep if j == 0 else (1.0 - keep).astype(BF16))
                dm = dot(xm, gt, NT)
                lc = l_sel[p, s0:s0 + sh, 64 * j:64 * j + 1]
                dc = d_sel[p, s0:s0 + sh, 64 * j:64 * j + 1]
                lr = l_t[2 * p + j][:, t0:]
                decay = jnp.exp(jnp.minimum(lr - lc, 0.0))
                gx.append(dot((decay * sm).astype(BF16), gt))
                dmd = dm * decay
                add = add + dmd * dc
                w = dmd * sm
                dr = dr + jnp.where(lane[:sh] == 2 * p + j, jnp.sum(w, axis=1, keepdims=True), 0.0)
                ce = jnp.concatenate(zero + [jnp.sum(w * dc, axis=0, keepdims=True)], axis=1)
                col_e[2 * p + j] = ce if s0 == 0 else col_e[2 * p + j] + ce
            direct[s0:s0 + sh, :] = dr
            dst[s0:s0 + sh, t0:] += add
            gxi[p, s0:s0 + sh, :] = jnp.where(low[:sh], gx[0], gx[1])

    def mixed(i, carry):
        chain_step(i - z * stride, z == 0, z == zn - 1, chain_f, own_f, sf, rf)
        chain_step(i - (zn - 1 - z) * stride, z == zn - 1, z == 0, chain_b, own_b, sb, rb)

        @pl.when(i < pairs)
        def _():
            local_pair(i)

        return carry

    lax.fori_loop(0, max(pairs, (zn - 1) * stride + chunks), mixed, 0)

    def carried(p, carry):
        cols = pl.ds(pl.multiple_of(p * LANES, LANES), LANES)
        entering, leaving = rf[p], rb[p]
        ls, ds = l_sel[p], d_sel[p]
        last = ls[tokens - 1:tokens, :]
        car = jnp.exp(ls) * g[:, cols].astype(F32) * dot(c_all, entering)
        br = jnp.exp(last - ls) * dot(b_all, leaving)
        gval[:, cols] = (ds * (gxi[p] + br)).astype(BF16)
        q = x[:, cols].astype(F32) * br
        ends = jnp.exp(last) * jnp.sum(entering.astype(F32) * leaving.astype(F32), axis=0, keepdims=True)
        q_new, c_new, e_new = qd[...], gl[...], fin[...]
        for j in range(2):
            mine, mine1 = (low, low1) if j == 0 else (~low, ~low1)
            at, at1 = lane == 2 * p + j, lane1 == 2 * p + j
            q_new = q_new + jnp.where(at, jnp.sum(jnp.where(mine, q, 0.0), axis=1, keepdims=True), 0.0)
            c_new = c_new + jnp.where(at, jnp.sum(jnp.where(mine, car, 0.0), axis=1, keepdims=True), 0.0)
            e_new = e_new + jnp.where(at1, jnp.sum(jnp.where(mine1, ends, 0.0), axis=1, keepdims=True), 0.0)
        qd[...], gl[...], fin[...] = q_new, c_new, e_new
        gacc[:, :state] += dot(xs[p], leaving, NT)
        gacc[:, state:] += dot(gs[p], entering, NT)
        return carry

    lax.fori_loop(0, pairs, carried, 0)

    d_masked = jnp.where(ti <= si, dst[...], 0.0).astype(BF16)
    px[hx, :, :state] = (gacc[:, :state] + dot(d_masked, c_all)).astype(BF16)
    px[hx, :, state:] = (gacc[:, state:] + dot(d_masked, b_all, TN)).astype(BF16)
    for k in range(1, hn):
        head_copies(k)[1].start()

    q_all = qd[...]
    straight = direct[...] + q_all
    for h in range(heads):
        erows[h:h + 1, :] = col_e[h]
    g_log = gl[...] + erows[...].T - delta * straight
    tail = jnp.sum(delta * q_all, axis=0, keepdims=True) + fin[...]
    back = dot_exact((ti <= si).astype(F32), g_log) + tail
    g_delta = straight + rate * back
    g_pre = g_delta * jax.nn.sigmoid(pre)
    smsend[...] = jnp.zeros_like(smsend)
    smsend[0:1, :] = jnp.sum(g_pre, axis=0, keepdims=True)
    smsend[1:2, :] = jnp.sum(delta * back, axis=0, keepdims=True) * rate
    gpx[hx] = g_pre.T[:rpad, :].astype(BF16)
    for k in range(1, hn):
        head_copies(k)[2].start()
    wsend[...] = dot(gpx[hx], uu).astype(BF16)

    other = {"batch": lax.rem(bt + 1, bn)}

    def core_copy(i, src, to):
        return pltpu.make_async_remote_copy(src, to, c_ss.at[i], c_rs.at[i], device_id=other, device_id_type=MESH)

    core_w = core_copy(0, wsend, wrecv)
    core_s = core_copy(1, smsend, smrecv)
    core_p = core_copy(2, csend, crecv)
    core_f = core_copy(3, wfsend, wfrecv)
    core_w.start()
    core_s.start()

    def along(i, src, to, k):
        there = lax.rem(z + k, zn)
        return pltpu.make_async_remote_copy(
            src, to.at[z], z_ss.at[i, k], z_rs.at[i, k], device_id={"tm": there}, device_id_type=MESH
        )

    def each_z(body):
        def turn(k, carry):
            body(k)
            return carry

        lax.fori_loop(1, zn, turn, 0)

    def z_start_small(k):
        along(0, wzsend, wzrecv, k).start()
        along(1, smzsend, smzrecv, k).start()

    def z_start_large(k):
        along(2, zsend.at[lax.rem(z + k, zn)], zrecv, k).start()

    def z_wait_small(k):
        along(0, wzsend, wzrecv, k).wait()
        along(1, smzsend, smzrecv, k).wait()

    def z_wait_large(k):
        along(2, zsend.at[lax.rem(z + k, zn)], zrecv, k).wait()

    for k in range(1, hn):
        for copy in head_copies(k):
            copy.wait()
    gp = px[0].astype(F32)
    for k in range(1, hn):
        gp = gp + px[k].astype(F32)
    gp = gp.astype(BF16)
    wide = zrecv.shape[2]
    if split:
        piece = jnp.where(hx == 0, gp[:, :wide], gp[:, wide:])
    else:
        piece = gp
    block = zrecv.shape[1]
    local = dot(uu, piece, TN)
    for k in range(zn * bn):
        plocal[k] = local[k * block:(k + 1) * block, :]
    for k in range(zn):
        csend[k] = plocal[k * bn + lax.rem(bt + 1, bn)].astype(BF16)
    core_p.start()

    core_w.wait()
    core_s.wait()
    wsum[...] = wsend[...].astype(F32) + wrecv[...].astype(F32)
    mine = pl.ds(pl.multiple_of(bt * half, LANES), half)
    theirs = pl.ds(pl.multiple_of(lax.rem(bt + 1, bn) * half, LANES), half)
    wz = wsum[:, mine].astype(BF16)
    wzsend[...] = wz
    wzrecv[z] = wz
    sz = smsend[...] + smrecv[...]
    smzsend[...] = sz
    smzrecv[z] = sz
    each_z(z_start_small)

    core_p.wait()
    for k in range(zn):
        zsend[k] = (plocal[k * bn + bt] + crecv[k].astype(F32)).astype(BF16)
    zrecv[z] = zsend[z]
    each_z(z_start_large)

    gpa = gpx[...].reshape(hn * rpad, tokens).astype(F32).T.astype(BF16)
    wa = wx[...].reshape(hn * rpad, width)
    gin[...] = (dot(gp, wbc[...], NT) + dot(gpa, wa)).astype(BF16)

    each_z(z_wait_small)
    total_w = wzrecv[0].astype(F32)
    total_s = smzrecv[0]
    for k in range(1, zn):
        total_w = total_w + wzrecv[k].astype(F32)
        total_s = total_s + smzrecv[k]
    wfsend[...] = total_w
    core_f.start()
    gsmall[...] = total_s
    gwdt[:, mine] = total_w

    each_z(z_wait_large)
    total = zrecv[0].astype(F32)
    for k in range(1, zn):
        total = total + zrecv[k].astype(F32)
    if split:
        fsend[...] = total
        final = pltpu.make_async_remote_copy(
            fsend, frecv, c_ss.at[4], c_rs.at[4], device_id={"head": lax.rem(hx + 1, hn)}, device_id_type=MESH
        )
        final.start()
        gwbc[:, pl.ds(pl.multiple_of(hx * wide, LANES), wide)] = total
        final.wait()
        gwbc[:, pl.ds(pl.multiple_of((1 - hx) * wide, LANES), wide)] = frecv[...]
    else:
        gwbc[...] = total
    core_f.wait()
    gwdt[:, theirs] = wfrecv[...]

    def drain(c, carry):
        @pl.when(z < zn - 1)
        def _():
            chain_f(c).wait_send()

        @pl.when(z > 0)
        def _():
            chain_b(c).wait_send()

        return carry

    lax.fori_loop(0, chunks, drain, 0)


def on_device(sizes, u_input, head_values, grad_output, w_bc, w_dt, dt_bias, a_log):
    zn, hn, bn = sizes
    seqs, tokens, width = u_input.shape
    assert seqs == 1 and bn == 2
    heads = w_dt.shape[1]
    values = head_values.shape[2]
    both = w_bc.shape[1]
    pairs = heads // 2
    assert values == heads * 64 and both == 2 * LANES and heads % 2 == 0
    split = hn == 2
    wide = both // 2 if split else both
    block = width // (zn * bn)
    rpad = -(-heads // 16) * 16
    half = width // bn
    chunks = pairs // 2 if pairs % 2 == 0 else pairs
    vm = pltpu.VMEM
    dma = pltpu.SemaphoreType.DMA
    scratch = [
        vm((width, LANES), BF16), vm((8, LANES), F32), vm((tokens, both), BF16), vm((heads, 1, tokens), F32),
        vm((pairs, tokens, LANES), F32), vm((pairs, tokens, LANES), F32),
        vm((pairs, tokens, LANES), BF16), vm((pairs, tokens, LANES), BF16),
        vm((pairs, LANES, LANES), F32), vm((pairs, LANES, LANES), F32), vm((pairs, tokens, LANES), F32),
        vm((tokens, tokens), F32), vm((tokens, tokens), F32), vm((heads, 1, tokens), F32), vm((LANES, tokens), F32),
        vm((tokens, LANES), F32), vm((tokens, LANES), F32), vm((tokens, LANES), F32), vm((1, LANES), F32),
        vm((tokens, both), F32),
        vm((pairs, LANES, LANES), BF16), vm((pairs, LANES, LANES), BF16),
        vm((pairs, LANES, LANES), BF16), vm((pairs, LANES, LANES), BF16),
        vm((hn, rpad, width), BF16), vm((hn, tokens, both), BF16), vm((hn, rpad, tokens), BF16),
        vm((zn, block, wide), BF16), vm((zn, block, wide), BF16), vm((zn * bn, block, wide), F32),
        vm((zn, block, wide), BF16), vm((zn, block, wide), BF16), vm((block, wide), F32), vm((block, wide), F32),
        vm((rpad, width), BF16), vm((rpad, width), BF16), vm((rpad, width), F32),
        vm((rpad, half), BF16), vm((zn, rpad, half), BF16), vm((rpad, half), F32), vm((rpad, half), F32),
        vm((8, LANES), F32), vm((8, LANES), F32), vm((8, LANES), F32), vm((zn, 8, LANES), F32),
        dma((chunks,)), dma((chunks,)), dma((chunks,)), dma((chunks,)),
        dma((3, hn)), dma((3, hn)), dma((5,)), dma((5,)), dma((3, zn)), dma((3, zn)),
    ]
    spec = pl.BlockSpec(memory_space=pltpu.VMEM)
    gin, gval, gwbc, gwdt, small = pl.pallas_call(
        functools.partial(kernel, zn, hn, bn, heads, split),
        out_shape=(
            jax.ShapeDtypeStruct((tokens, width), BF16),
            jax.ShapeDtypeStruct((tokens, values), BF16),
            jax.ShapeDtypeStruct((block, both), F32),
            jax.ShapeDtypeStruct((rpad, width), F32),
            jax.ShapeDtypeStruct((8, LANES), F32),
        ),
        in_specs=[spec] * 7,
        out_specs=[spec] * 5,
        scratch_shapes=scratch,
        compiler_params=pltpu.CompilerParams(
            collective_id=0, has_side_effects=True, vmem_limit_bytes=56 << 20
        ),
    )(
        u_input.reshape(tokens, width), head_values.reshape(tokens, values), grad_output.reshape(tokens, values),
        w_bc, w_dt, dt_bias.reshape(1, heads), a_log.reshape(1, heads),
    )
    return (
        gin.reshape(1, tokens, width), gval.reshape(1, tokens, values), gwbc,
        gwdt[:heads].T, small[0, :heads], small[1, :heads],
    )


def solution(mesh):
    sizes = (mesh.shape["tm"], mesh.shape["head"], mesh.shape["batch"])
    return jax.shard_map(
        functools.partial(on_device, sizes),
        mesh=mesh,
        in_specs=(
            P(("groups", "batch"), "tm", None),
            P(("groups", "batch"), "tm", "head"),
            P(("groups", "batch"), "tm", "head"),
            P(),
            P(None, "head"),
            P("head"),
            P("head"),
        ),
        out_specs=(
            P(("groups", "batch"), "tm", None),
            P(("groups", "batch"), "tm", "head"),
            P(("groups", "tm", "batch"), None),
            P("groups", "head"),
            P(("groups", "head")),
            P(("groups", "head")),
        ),
        check_vma=False,
    )
```

time: 289 us -> 60.8 us (0.21)
  waiting for transfers between devices: 140 us -> 0 us
  Pallas kernels: 0 us -> 51.3 us
  blocking collectives: 47.8 us -> 0 us
  matrix products: 33.6 us -> 0 us
  local copies, waits for them, and re-layouts: 30 us -> 8.58 us
  other arithmetic: 21.3 us -> 0 us
  between operations: 14.1 us -> 0.64 us
    all_gather x2 -> x0, waiting for transfers between devices: 90.5 us -> none  [prefix(): everything = jax.tree.map(lambda part: lax.all_gather(part, axis), shard)]
    pallas_call x0 -> x1, Pallas kernels: none -> 51.3 us  [on_device(): pl.pallas_call(functools.partial(kernel, zn, hn, bn, heads, split), out_s...]
    unnamed x5 -> x0, waiting for transfers between devices: 38.5 us -> none
    dot_general x17 -> x0, matrix products: 33.6 us -> none  [the longest x2 12.4 us: span_core(): inner = jnp.einsum('hts,shp->thp', mixing, values_in, precision=highest)]
    psum x2 -> x0, blocking collectives: 25.6 us -> none  [the longest x1 14.1 us: on_device(): lax.psum((local_w_dt, jnp.sum(grad_pre, axis=0), jnp.sum(g_rate, axis=0)...]
    all_gather x3 -> x0, blocking collectives: 22.2 us -> none  [the longest x1 12.8 us: prefix(): everything = jax.tree.map(lambda part: lax.all_gather(part, axis), shard)]
    psum x1 -> x0, waiting for transfers between devices: 10.8 us -> none  [on_device(): lax.psum((local_w_dt, jnp.sum(grad_pre, axis=0), jnp.sum(g_rate, axis=0)...]
    select_n x8 -> x0, other arithmetic: 10.4 us -> none  [turn(): return jax.tree.map(lambda a, b: jnp.where(reached, a, b), new, before)]
  transfers between devices with their start and end apart: 4 -> 0, of which waited for: 4 -> 0; matrix products, arithmetic and copies ran while one was open for 14% -> 0% of each run, Pallas kernels for 0% -> 0%
where the time goes in v1:
time: 60.8 us; the launch traced here: 60.5 us
  Pallas kernels  51.3 us (84%)
  local copies, waits for them, and re-layouts  8.58 us (14%)
  between operations  0.64 us (1%)
    pallas_call x1, Pallas kernels, on_device(): pl.pallas_call(functools.partial(kernel, zn, hn, bn, heads, split), out_s...  51.3 us
    unnamed x8, local copies, waits for them, and re-layouts  5.74 us
    transpose x1, local copies, waits for them, and re-layouts, on_device(): gwdt[:heads]  1.58 us
    squeeze x1, local copies, waits for them, and re-layouts, on_device(): small[1, :heads]  1.26 us

profile of v1, /device:TPU:0, one launch (start us, length us, event | category | flops | bytes accessed | tf_op | source)
XLA Modules:
  0.0 60.5 jit_solution(1611850590343746116)
XLA Ops:
  0.6 1.8 %copy.13.wdt = bf16[1536,24]{1,0:T(8,128)(2,1)} copy(bf16[1536,24]{0,1:T(8,128)(2,1)} %param.11) | data formatting | bytes 147456 | tf_op args[4]
  2.4 51.3 %shard_map.118 = (bf16[256,1536]{1,0:T(8,128)(2,1)}, bf16[256,1536]{1,0:T(8,128)(2,1)}, f32[192,256]{1,0:T(8,128)}, f32[32,1536]{1,0:T(8,128)}, f32[8,128]{1,0:T(8,128)}) custom-call(bf16[256,1536]{1,0:T(8,128)(2,1)} %bitcast.15, bf16[256,1536]{1,0:T(8,128)(2,1)} %bitcast.16, bf16[256,1536]{1,0:T(8,128)(2,1)} %bitcast.17, bf16[1536,256]{1,0:T(8,128)(2,1)} %wbc.1, ...), custom_call_target="tpu_custom_call" | custom-call | tf_op jit(solution)/shard_map/pallas_call | solution.py:420
  53.7 1.3 %slice_bitcast_fusion.1 = (f32[24]{0:T(128)}, f32[24]{0:T(128)}) fusion(f32[8,128]{1,0:T(8,128)} %get-tuple-element.15), kind=kLoop, calls=%fused_computation.1 | loop fusion | bytes 384 | tf_op jit(solution)/shard_map/squeeze | solution.py:441
  55.0 1.6 %slice_bitcast_fusion = f32[1536,24]{0,1:T(8,128)} fusion(f32[32,1536]{1,0:T(8,128)} %get-tuple-element.14), kind=kLoop, calls=%fused_computation | loop fusion | bytes 294912 | tf_op jit(solution)/shard_map/transpose | solution.py:441
  56.6 0.0 copy-start
  56.6 2.1 %copy.17 = bf16[1,256,1536]{2,1,0:T(8,128)(2,1)} copy(bf16[1,256,1536]{2,1,0:T(8,128)(2,1)} %bitcast.14) | data formatting | bytes 1572864
  58.7 0.0 copy-done
  58.7 0.0 copy-start.1
  58.7 0.9 %copy.18 = bf16[1,256,1536]{2,1,0:T(8,128)(2,1)} copy(bf16[1,256,1536]{2,1,0:T(8,128)(2,1)S(1)} %bitcast.13) | data formatting | bytes 1572864
  59.6 0.2 copy-done.1
  59.8 0.7 %copy.19 = f32[192,256]{1,0:T(8,128)} copy(f32[192,256]{1,0:T(8,128)S(1)} %copy-done.1) | data formatting | bytes 393216
Async XLA Ops:
  56.6 2.1 %copy-start = (bf16[256,1536]{1,0:T(8,128)(2,1)S(1)}, bf16[256,1536]{1,0:T(8,128)(2,1)}, u32[]{:S(2)}) copy-start(bf16[256,1536]{1,0:T(8,128)(2,1)} %get-tuple-element.12) | copy-start | bytes 2359300
  58.7 1.1 %copy-start.1 = (f32[192,256]{1,0:T(8,128)S(1)}, f32[192,256]{1,0:T(8,128)}, u32[]{:S(2)}) copy-start(f32[192,256]{1,0:T(8,128)} %get-tuple-element.26) | copy-start | bytes 589828

commit v2 on v1

--- a/solution.py
+++ b/solution.py
@@ -29,8 +29,8 @@
 def kernel(
     zn, hn, bn, heads, split,
     u, x, g, wbc, wdt, bias, alog,
-    gin, gval, gwbc, gwdt, gsmall,
-    wpad, rows, proj, l_t, l_sel, d_sel, xs, gs, own_f, own_b, gxi, st, dst, col_e, erows,
+    gin, gval, gwbc, gwdt, gbias, galog,
+    wpad, ut, rows, proj, l_t, l_sel, d_sel, xs, gs, own_f, own_b, gxi, st, dst, col_e, erows,
     direct, qd, gl, fin, gacc,
     sf, rf, sb, rb, wx, px, gpx, csend, crecv, plocal, zsend, zrecv, fsend, frecv,
     wsend, wrecv, wsum, wzsend, wzrecv, wfsend, wfrecv, smsend, smrecv, smzsend, smzrecv,
@@ -59,13 +59,13 @@
         pl.semaphore_signal(barrier, inc=1, device_id={"batch": lax.rem(bt + k, bn)}, device_id_type=MESH)
 
     wpad[...] = jnp.zeros_like(wpad)
-    wpad[:, :heads] = wdt[...]
+    wpad[:heads, :] = wdt[...]
     rows[...] = jnp.zeros_like(rows)
     rows[0:1, :heads] = bias[...]
     rows[1:2, :heads] = alog[...]
     uu = u[...]
     proj[...] = dot(uu, wbc[...]).astype(BF16)
-    pre = dot(uu, wpad[...]) + rows[0:1, :]
+    pre = dot(uu, wpad[...], NT) + rows[0:1, :]
     delta = jnp.maximum(pre, 0.0) + jnp.log1p(jnp.exp(-jnp.abs(pre)))
     rate = -jnp.exp(rows[1:2, :])
     ti = lax.broadcasted_iota(jnp.int32, (tokens, tokens), 0)
@@ -78,11 +78,7 @@
     b_t = b_all.astype(F32).T.astype(BF16)
     c_t = c_all.astype(F32).T.astype(BF16)
     st[...] = jnp.where(ti <= si, dot(b_all, c_all, NT), 0.0)
-    ident = (
-        lax.broadcasted_iota(jnp.int32, (rpad, LANES), 0)
-        == lax.broadcasted_iota(jnp.int32, (rpad, LANES), 1)
-    ).astype(BF16)
-    wx[hx] = dot(ident, wpad[...], NT).astype(BF16)
+    wx[hx] = wpad[:rpad, :]
 
     def pick(value, head):
         return jnp.sum(jnp.where(lane == head, value, 0.0), axis=1, keepdims=True)
@@ -294,6 +290,10 @@
     def z_wait_large(k):
         along(2, zsend.at[lax.rem(z + k, zn)], zrecv, k).wait()
 
+    for k in range(width // 256):
+        at = k * 256
+        ut[at:at + 256, :] = u[:, at:at + 256].astype(F32).T.astype(BF16)
+
     for k in range(1, hn):
         for copy in head_copies(k):
             copy.wait()
@@ -307,7 +307,7 @@
     else:
         piece = gp
     block = zrecv.shape[1]
-    local = dot(uu, piece, TN)
+    local = dot(ut[...], piece)
     for k in range(zn * bn):
         plocal[k] = local[k * block:(k + 1) * block, :]
     for k in range(zn):
@@ -345,8 +345,9 @@
         total_s = total_s + smzrecv[k]
     wfsend[...] = total_w
     core_f.start()
-    gsmall[...] = total_s
-    gwdt[:, mine] = total_w
+    gbias[...] = total_s[0:1, :heads]
+    galog[...] = total_s[1:2, :heads]
+    gwdt[:, mine] = total_w[:heads, :]
 
     each_z(z_wait_large)
     total = zrecv[0].astype(F32)
@@ -364,7 +365,7 @@
     else:
         gwbc[...] = total
     core_f.wait()
-    gwdt[:, theirs] = wfrecv[...]
+    gwdt[:, theirs] = wfrecv[:heads, :]
 
     def drain(c, carry):
         @pl.when(z < zn - 1)
@@ -398,7 +399,7 @@
     vm = pltpu.VMEM
     dma = pltpu.SemaphoreType.DMA
     scratch = [
-        vm((width, LANES), BF16), vm((8, LANES), F32), vm((tokens, both), BF16), vm((heads, 1, tokens), F32),
+        vm((LANES, width), BF16), vm((width, tokens), BF16), vm((8, LANES), F32), vm((tokens, both), BF16), vm((heads, 1, tokens), F32),
         vm((pairs, tokens, LANES), F32), vm((pairs, tokens, LANES), F32),
         vm((pairs, tokens, LANES), BF16), vm((pairs, tokens, LANES), BF16),
         vm((pairs, LANES, LANES), F32), vm((pairs, LANES, LANES), F32), vm((pairs, tokens, LANES), F32),
@@ -417,28 +418,29 @@
         dma((3, hn)), dma((3, hn)), dma((5,)), dma((5,)), dma((3, zn)), dma((3, zn)),
     ]
     spec = pl.BlockSpec(memory_space=pltpu.VMEM)
-    gin, gval, gwbc, gwdt, small = pl.pallas_call(
+    gin, gval, gwbc, gwdt, gbias, galog = pl.pallas_call(
         functools.partial(kernel, zn, hn, bn, heads, split),
         out_shape=(
             jax.ShapeDtypeStruct((tokens, width), BF16),
             jax.ShapeDtypeStruct((tokens, values), BF16),
             jax.ShapeDtypeStruct((block, both), F32),
-            jax.ShapeDtypeStruct((rpad, width), F32),
-            jax.ShapeDtypeStruct((8, LANES), F32),
+            jax.ShapeDtypeStruct((heads, width), F32),
+            jax.ShapeDtypeStruct((1, heads), F32),
+            jax.ShapeDtypeStruct((1, heads), F32),
         ),
         in_specs=[spec] * 7,
-        out_specs=[spec] * 5,
+        out_specs=[spec] * 6,
         scratch_shapes=scratch,
         compiler_params=pltpu.CompilerParams(
             collective_id=0, has_side_effects=True, vmem_limit_bytes=56 << 20
         ),
     )(
         u_input.reshape(tokens, width), head_values.reshape(tokens, values), grad_output.reshape(tokens, values),
-        w_bc, w_dt, dt_bias.reshape(1, heads), a_log.reshape(1, heads),
+        w_bc, w_dt.T, dt_bias.reshape(1, heads), a_log.reshape(1, heads),
     )
     return (
         gin.reshape(1, tokens, width), gval.reshape(1, tokens, values), gwbc,
-        gwdt[:heads].T, small[0, :heads], small[1, :heads],
+        gwdt.T, gbias.reshape(heads), galog.reshape(heads),
     )
 
 

time: 60.8 us -> 58.2 us (0.957)
  local copies, waits for them, and re-layouts: 8.58 us -> 6.07 us
    transpose x1 -> x0, local copies, waits for them, and re-layouts: 1.58 us -> none  [on_device(): gwdt[:heads]]
    squeeze x1 -> x0, local copies, waits for them, and re-layouts: 1.26 us -> none  [on_device(): small[1, :heads]]
    unnamed x8 -> x16, local copies, waits for them, and re-layouts: 5.74 us -> 6.07 us
where the time goes in v2:
time: 58.2 us; the launch traced here: 58 us
  Pallas kernels  51.2 us (88%)
  local copies, waits for them, and re-layouts  6.07 us (10%)
  between operations  0.66 us (1%)
    pallas_call x1, Pallas kernels, on_device(): pl.pallas_call(functools.partial(kernel, zn, hn, bn, heads, split), out_s...  51.2 us
    unnamed x16, local copies, waits for them, and re-layouts  6.07 us

profile of v2, /device:TPU:0, one launch (start us, length us, event | category | flops | bytes accessed | tf_op | source)
XLA Modules:
  0.0 58.0 jit_solution(8866196655792408272)
XLA Ops:
  0.6 51.2 %shard_map.118 = (bf16[256,1536]{1,0:T(8,128)(2,1)}, bf16[256,1536]{1,0:T(8,128)(2,1)}, f32[192,256]{1,0:T(8,128)}, f32[24,1536]{1,0:T(8,128)}, f32[1,24]{1,0:T(1,128)}, /*index=5*/f32[1,24]{1,0:T(1,128)}) custom-call(bf16[256,1536]{1,0:T(8,128)(2,1)} %bitcast.13, bf16[256,1536]{1,0:T(8,128)(2,1)} %bitcast.14, bf16[256,1536]{1,0:T(8,128)(2,1)} %bitcast.15, ...), custom_call_target="tpu_custom_call" | custom-call | tf_op jit(solution)/shard_map/pallas_call | solution.py:421
  51.9 0.0 copy-start
  51.9 2.1 %copy.19 = bf16[1,256,1536]{2,1,0:T(8,128)(2,1)} copy(bf16[1,256,1536]{2,1,0:T(8,128)(2,1)} %bitcast.12) | data formatting | bytes 1572864
  54.0 0.0 copy-done
  54.0 0.0 copy-start.1
  54.0 0.9 %copy.20 = bf16[1,256,1536]{2,1,0:T(8,128)(2,1)} copy(bf16[1,256,1536]{2,1,0:T(8,128)(2,1)S(1)} %bitcast.11) | data formatting | bytes 1572864
  54.9 0.2 copy-done.1
  55.1 0.0 copy-start.2
  55.1 0.7 %copy.21 = f32[192,256]{1,0:T(8,128)} copy(f32[192,256]{1,0:T(8,128)S(1)} %copy-done.1) | data formatting | bytes 393216
  55.8 0.3 copy-done.2
  56.1 0.0 copy-start.4
  56.1 0.7 %copy.22 = f32[1536,24]{0,1:T(8,128)} copy(f32[1536,24]{0,1:T(8,128)S(1)} %bitcast.16) | data formatting | bytes 294912
  56.8 0.0 copy-done.4
  56.8 0.0 copy-start.3
  56.8 0.5 copy.23
  57.3 0.1 copy-done.3
  57.5 0.5 copy.24
Async XLA Ops:
  51.9 2.1 %copy-start = (bf16[256,1536]{1,0:T(8,128)(2,1)S(1)}, bf16[256,1536]{1,0:T(8,128)(2,1)}, u32[]{:S(2)}) copy-start(bf16[256,1536]{1,0:T(8,128)(2,1)} %get-tuple-element.13) | copy-start | bytes 2359300
  54.0 1.1 %copy-start.1 = (f32[192,256]{1,0:T(8,128)S(1)}, f32[192,256]{1,0:T(8,128)}, u32[]{:S(2)}) copy-start(f32[192,256]{1,0:T(8,128)} %get-tuple-element.26) | copy-start | bytes 589828
  55.1 1.0 %copy-start.2 = (f32[24,1536]{1,0:T(8,128)S(1)}, f32[24,1536]{1,0:T(8,128)}, u32[]{:S(2)}) copy-start(f32[24,1536]{1,0:T(8,128)} %get-tuple-element.15) | copy-start | bytes 442372
  56.1 0.7 %copy-start.4 = (f32[1,24]{1,0:T(1,128)S(1)}, f32[1,24]{1,0:T(1,128)}, u32[]{:S(2)}) copy-start(f32[1,24]{1,0:T(1,128)} %get-tuple-element.16) | copy-start | bytes 292
  56.8 0.7 %copy-start.3 = (f32[1,24]{1,0:T(1,128)S(1)}, f32[1,24]{1,0:T(1,128)}, u32[]{:S(2)}) copy-start(f32[1,24]{1,0:T(1,128)} %get-tuple-element.17) | copy-start | bytes 292

commit v3 on v2

--- a/solution.py
+++ b/solution.py
@@ -294,6 +294,19 @@
         at = k * 256
         ut[at:at + 256, :] = u[:, at:at + 256].astype(F32).T.astype(BF16)
 
+    core_w.wait()
+    core_s.wait()
+    wsum[...] = wsend[...].astype(F32) + wrecv[...].astype(F32)
+    mine = pl.ds(pl.multiple_of(bt * half, LANES), half)
+    theirs = pl.ds(pl.multiple_of(lax.rem(bt + 1, bn) * half, LANES), half)
+    wz = wsum[:, mine].astype(BF16)
+    wzsend[...] = wz
+    wzrecv[z] = wz
+    sz = smsend[...] + smrecv[...]
+    smzsend[...] = sz
+    smzrecv[z] = sz
+    each_z(z_start_small)
+
     for k in range(1, hn):
         for copy in head_copies(k):
             copy.wait()
@@ -313,19 +326,6 @@
     for k in range(zn):
         csend[k] = plocal[k * bn + lax.rem(bt + 1, bn)].astype(BF16)
     core_p.start()
-
-    core_w.wait()
-    core_s.wait()
-    wsum[...] = wsend[...].astype(F32) + wrecv[...].astype(F32)
-    mine = pl.ds(pl.multiple_of(bt * half, LANES), half)
-    theirs = pl.ds(pl.multiple_of(lax.rem(bt + 1, bn) * half, LANES), half)
-    wz = wsum[:, mine].astype(BF16)
-    wzsend[...] = wz
-    wzrecv[z] = wz
-    sz = smsend[...] + smrecv[...]
-    smzsend[...] = sz
-    smzrecv[z] = sz
-    each_z(z_start_small)
 
     core_p.wait()
     for k in range(zn):

time: 58.2 us -> 57.4 us (0.986)
  Pallas kernels: 51.2 us -> 50.4 us
    pallas_call x1, Pallas kernels: 51.2 us -> 50.4 us  [on_device(): pl.pallas_call(functools.partial(kernel, zn, hn, bn, heads, split), out_s...]
where the time goes in v3:
time: 57.4 us; the launch traced here: 57.1 us
  Pallas kernels  50.4 us (88%)
  local copies, waits for them, and re-layouts  6.07 us (11%)
  between operations  0.66 us (1%)
    pallas_call x1, Pallas kernels, on_device(): pl.pallas_call(functools.partial(kernel, zn, hn, bn, heads, split), out_s...  50.4 us
    unnamed x16, local copies, waits for them, and re-layouts  6.07 us

profile of v3, /device:TPU:0, one launch (start us, length us, event | category | flops | bytes accessed | tf_op | source)
XLA Modules:
  0.0 57.1 jit_solution(12671993715086022556)
XLA Ops:
  0.6 50.4 %shard_map.118 = (bf16[256,1536]{1,0:T(8,128)(2,1)}, bf16[256,1536]{1,0:T(8,128)(2,1)}, f32[192,256]{1,0:T(8,128)}, f32[24,1536]{1,0:T(8,128)}, f32[1,24]{1,0:T(1,128)}, /*index=5*/f32[1,24]{1,0:T(1,128)}) custom-call(bf16[256,1536]{1,0:T(8,128)(2,1)} %bitcast.13, bf16[256,1536]{1,0:T(8,128)(2,1)} %bitcast.14, bf16[256,1536]{1,0:T(8,128)(2,1)} %bitcast.15, ...), custom_call_target="tpu_custom_call" | custom-call | tf_op jit(solution)/shard_map/pallas_call | solution.py:421
  51.0 0.0 copy-start
  51.0 2.1 %copy.19 = bf16[1,256,1536]{2,1,0:T(8,128)(2,1)} copy(bf16[1,256,1536]{2,1,0:T(8,128)(2,1)} %bitcast.12) | data formatting | bytes 1572864
  53.2 0.0 copy-done
  53.2 0.0 copy-start.1
  53.2 0.9 %copy.20 = bf16[1,256,1536]{2,1,0:T(8,128)(2,1)} copy(bf16[1,256,1536]{2,1,0:T(8,128)(2,1)S(1)} %bitcast.11) | data formatting | bytes 1572864
  54.1 0.2 copy-done.1
  54.3 0.0 copy-start.2
  54.3 0.7 %copy.21 = f32[192,256]{1,0:T(8,128)} copy(f32[192,256]{1,0:T(8,128)S(1)} %copy-done.1) | data formatting | bytes 393216
  55.0 0.3 copy-done.2
  55.3 0.0 copy-start.4
  55.3 0.7 %copy.22 = f32[1536,24]{0,1:T(8,128)} copy(f32[1536,24]{0,1:T(8,128)S(1)} %bitcast.16) | data formatting | bytes 294912
  55.9 0.0 copy-done.4
  56.0 0.0 copy-start.3
  56.0 0.5 copy.23
  56.5 0.1 copy-done.3
  56.6 0.5 copy.24
Async XLA Ops:
  51.0 2.1 %copy-start = (bf16[256,1536]{1,0:T(8,128)(2,1)S(1)}, bf16[256,1536]{1,0:T(8,128)(2,1)}, u32[]{:S(2)}) copy-start(bf16[256,1536]{1,0:T(8,128)(2,1)} %get-tuple-element.13) | copy-start | bytes 2359300
  53.2 1.1 %copy-start.1 = (f32[192,256]{1,0:T(8,128)S(1)}, f32[192,256]{1,0:T(8,128)}, u32[]{:S(2)}) copy-start(f32[192,256]{1,0:T(8,128)} %get-tuple-element.26) | copy-start | bytes 589828
  54.3 1.0 %copy-start.2 = (f32[24,1536]{1,0:T(8,128)S(1)}, f32[24,1536]{1,0:T(8,128)}, u32[]{:S(2)}) copy-start(f32[24,1536]{1,0:T(8,128)} %get-tuple-element.15) | copy-start | bytes 442372
  55.3 0.7 %copy-start.4 = (f32[1,24]{1,0:T(1,128)S(1)}, f32[1,24]{1,0:T(1,128)}, u32[]{:S(2)}) copy-start(f32[1,24]{1,0:T(1,128)} %get-tuple-element.16) | copy-start | bytes 292
  56.0 0.7 %copy-start.3 = (f32[1,24]{1,0:T(1,128)S(1)}, f32[1,24]{1,0:T(1,128)}, u32[]{:S(2)}) copy-start(f32[1,24]{1,0:T(1,128)} %get-tuple-element.17) | copy-start | bytes 292

commit v4 on v3

--- a/solution.py
+++ b/solution.py
@@ -45,6 +45,12 @@
     state = LANES
     rpad = wx.shape[1]
     half = width // bn
+
+    def several(body, i, carry):
+        for j in range(per):
+            carry = body(i * per + j, carry)
+        return carry
+
     lane = lax.broadcasted_iota(jnp.int32, (tokens, LANES), 1)
     lane1 = lax.broadcasted_iota(jnp.int32, (1, LANES), 1)
     low = lane < 64
@@ -97,7 +103,7 @@
         own_b[p] = dot(c_t, gv)
         return carry
 
-    lax.fori_loop(0, pairs, summarize, 0)
+    lax.fori_loop(0, pairs // per, lambda i, carry: several(summarize, i, carry), 0)
 
     dst[...] = jnp.zeros_like(dst)
     erows[...] = jnp.zeros_like(erows)
@@ -226,7 +232,7 @@
         gacc[:, state:] += dot(gs[p], entering, NT)
         return carry
 
-    lax.fori_loop(0, pairs, carried, 0)
+    lax.fori_loop(0, pairs // per, lambda i, carry: several(carried, i, carry), 0)
 
     d_masked = jnp.where(ti <= si, dst[...], 0.0).astype(BF16)
     px[hx, :, :state] = (gacc[:, :state] + dot(d_masked, c_all)).astype(BF16)

time: 57.4 us -> 54.8 us (0.955)
  Pallas kernels: 50.4 us -> 47.8 us
    pallas_call x1, Pallas kernels: 50.4 us -> 47.8 us  [on_device(): pl.pallas_call(functools.partial(kernel, zn, hn, bn, heads, split), out_s...]
where the time goes in v4:
time: 54.8 us; the launch traced here: 54.6 us
  Pallas kernels  47.8 us (87%)
  local copies, waits for them, and re-layouts  6.07 us (11%)
  between operations  0.66 us (1%)
    pallas_call x1, Pallas kernels, on_device(): pl.pallas_call(functools.partial(kernel, zn, hn, bn, heads, split), out_s...  47.8 us
    unnamed x16, local copies, waits for them, and re-layouts  6.07 us

profile of v4, /device:TPU:0, one launch (start us, length us, event | category | flops | bytes accessed | tf_op | source)
XLA Modules:
  0.0 54.6 jit_solution(4747939176929512252)
XLA Ops:
  0.6 47.8 %shard_map.118 = (bf16[256,1536]{1,0:T(8,128)(2,1)}, bf16[256,1536]{1,0:T(8,128)(2,1)}, f32[192,256]{1,0:T(8,128)}, f32[24,1536]{1,0:T(8,128)}, f32[1,24]{1,0:T(1,128)}, /*index=5*/f32[1,24]{1,0:T(1,128)}) custom-call(bf16[256,1536]{1,0:T(8,128)(2,1)} %bitcast.13, bf16[256,1536]{1,0:T(8,128)(2,1)} %bitcast.14, bf16[256,1536]{1,0:T(8,128)(2,1)} %bitcast.15, ...), custom_call_target="tpu_custom_call" | custom-call | tf_op jit(solution)/shard_map/pallas_call | solution.py:427
  48.5 0.0 copy-start
  48.5 2.1 %copy.19 = bf16[1,256,1536]{2,1,0:T(8,128)(2,1)} copy(bf16[1,256,1536]{2,1,0:T(8,128)(2,1)} %bitcast.12) | data formatting | bytes 1572864
  50.6 0.0 copy-done
  50.6 0.0 copy-start.1
  50.6 0.9 %copy.20 = bf16[1,256,1536]{2,1,0:T(8,128)(2,1)} copy(bf16[1,256,1536]{2,1,0:T(8,128)(2,1)S(1)} %bitcast.11) | data formatting | bytes 1572864
  51.5 0.2 copy-done.1
  51.7 0.0 copy-start.2
  51.7 0.7 %copy.21 = f32[192,256]{1,0:T(8,128)} copy(f32[192,256]{1,0:T(8,128)S(1)} %copy-done.1) | data formatting | bytes 393216
  52.4 0.3 copy-done.2
  52.7 0.0 copy-start.4
  52.7 0.7 %copy.22 = f32[1536,24]{0,1:T(8,128)} copy(f32[1536,24]{0,1:T(8,128)S(1)} %bitcast.16) | data formatting | bytes 294912
  53.4 0.0 copy-done.4
  53.4 0.0 copy-start.3
  53.4 0.5 copy.23
  53.9 0.1 copy-done.3
  54.0 0.5 copy.24
Async XLA Ops:
  48.5 2.1 %copy-start = (bf16[256,1536]{1,0:T(8,128)(2,1)S(1)}, bf16[256,1536]{1,0:T(8,128)(2,1)}, u32[]{:S(2)}) copy-start(bf16[256,1536]{1,0:T(8,128)(2,1)} %get-tuple-element.13) | copy-start | bytes 2359300
  50.6 1.1 %copy-start.1 = (f32[192,256]{1,0:T(8,128)S(1)}, f32[192,256]{1,0:T(8,128)}, u32[]{:S(2)}) copy-start(f32[192,256]{1,0:T(8,128)} %get-tuple-element.26) | copy-start | bytes 589828
  51.7 1.0 %copy-start.2 = (f32[24,1536]{1,0:T(8,128)S(1)}, f32[24,1536]{1,0:T(8,128)}, u32[]{:S(2)}) copy-start(f32[24,1536]{1,0:T(8,128)} %get-tuple-element.15) | copy-start | bytes 442372
  52.7 0.7 %copy-start.4 = (f32[1,24]{1,0:T(1,128)S(1)}, f32[1,24]{1,0:T(1,128)}, u32[]{:S(2)}) copy-start(f32[1,24]{1,0:T(1,128)} %get-tuple-element.16) | copy-start | bytes 292
  53.4 0.7 %copy-start.3 = (f32[1,24]{1,0:T(1,128)S(1)}, f32[1,24]{1,0:T(1,128)}, u32[]{:S(2)}) copy-start(f32[1,24]{1,0:T(1,128)} %get-tuple-element.17) | copy-start | bytes 292
